TPU v7x, 32 devices: a whole 2x2x4 slice. The times are simulated.
32 devices in a mesh: dp: 8 (over z, core), tensor: 4 (over y, x).
Axes of the slice: x: 2, y: 2, z: 4, core: 2. Of those that a mesh axis runs over, the one named last changes fastest.
Arguments:
- inputs: bfloat16 [12288, 2048], P(('dp', 'tensor')), may hold values from -6 to 6
- cotangent: bfloat16 [12288, 2048], P(('dp', 'tensor')), may hold values from -6 to 6
- routes: int32 [12288, 4], P('dp'), may hold values from 0 to 15, all different within a row; in each aligned block of 1536 rows (0 to 1535, 1536 to 3071, ...) at most 408 rows name the same one
- gain_attn: float32 [2048], replicated, may hold values from 0.5 to 1.5
- w_qkv: float32 [2048, 3, 2048], P('dp', None, 'tensor'), may hold values from -0.125 to 0.125
- qkv_bias: float32 [3, 16, 128], P(None, 'tensor', 'dp'), may hold values from -0.6 to 0.6
- w_out: float32 [2048, 2048], P('dp', 'tensor'), may hold values from -1 to 1
- gain_ffn: float32 [2048], replicated, may hold values from 0.5 to 1.5
- router: float32 [16, 2048], replicated, may hold values from -0.0625 to 0.0625
- shared_gate: float32 [2048], replicated, may hold values from -0.125 to 0.125
- expert_gate_up: float32 [16, 2, 1408, 2048], P(None, None, 'tensor', 'dp'), may hold values from -0.125 to 0.125
- expert_down: float32 [16, 1408, 2048], P(None, 'tensor', 'dp'), may hold values from -2.5 to 2.5
- shared_gate_up: float32 [2048, 2, 5632], P('dp', None, 'tensor'), may hold values from -0.125 to 0.125
- shared_down: float32 [2048, 5632], P('dp', 'tensor'), may hold values from -0.15625 to 0.15625
Outputs:
- layer_out: bfloat16 [12288, 2048], P(('dp', 'tensor'))
- input_grad: float32 [12288, 2048], P(('dp', 'tensor'))
- gain_attn_grad: float32 [2048], P(('dp', 'tensor'))
- w_qkv_grad: float32 [2048, 3, 2048], P('dp', None, 'tensor')
- qkv_bias_grad: float32 [3, 16, 128], P(None, 'tensor', 'dp')
- w_out_grad: float32 [2048, 2048], P('dp', 'tensor')
- gain_ffn_grad: float32 [2048], P(('dp', 'tensor'))
- router_grad: float32 [16, 2048], P(None, ('dp', 'tensor'))
- shared_gate_grad: float32 [2048], P(('dp', 'tensor'))
- expert_gate_up_grad: float32 [16, 2, 1408, 2048], P(None, None, 'tensor', 'dp')
- expert_down_grad: float32 [16, 1408, 2048], P(None, 'tensor', 'dp')
- shared_gate_up_grad: float32 [2048, 2, 5632], P('dp', None, 'tensor')
- shared_down_grad: float32 [2048, 5632], P('dp', 'tensor')
Inputs may be any that keep to these rules, and one draw needn't show every extreme that they name: `routes`: in each block of 1536 rows held by one index of dp, every row names 4 different experts, no expert is named by more than 408 rows, a bound that some block reaches.
All inputs are finite; a program needn't handle non-finite values.
Results may differ from a plain program's by a relative error of at most 0.023.
Values may be sent and summed in bfloat16 or wider, within the bound.
No kernel may reach another device: no remote copies, remote signals or barrier semaphores. Data moves between devices by JAX's collectives and lax.ppermute only.
A program may use at most 384 MiB of HBM per device.

v0:
```python
import jax
import jax.numpy as jnp
from jax import lax
from jax.sharding import PartitionSpec as P

TOP = 4
EXPERTS = 16
PROMPT = 2048
CONT = 256
CONTS = 4
QBLOCK = 512
BLOCK = 1536
CAP = 408


EPSILON = 1e-06
ROPE_BASE = 1000000.0
MASKED = -1000000000.0
HIGHEST = lax.Precision.HIGHEST


def from_partner(value, axis, distance):
    mask = 2**distance
    pairs = [(source, source ^ mask) for source in range(lax.axis_size(axis))]
    return lax.ppermute(value, axis, pairs)


def block_layout(half_index):
    row_ids = jnp.arange(BLOCK, dtype=jnp.int32)
    half_len = PROMPT // 2
    offset = row_ids - half_len
    in_prompt = row_ids < half_len
    positions = jnp.where(in_prompt, half_index * half_len + row_ids, PROMPT + offset % CONT)
    segment = jnp.where(in_prompt, -1, half_index * (CONTS // 2) + offset // CONT)
    return (positions, segment)


def rotary(tensor_in, positions, direction):
    half_dim = tensor_in.shape[-1] // 2
    frequency = ROPE_BASE ** (
        -(jnp.arange(half_dim, dtype=jnp.float32) * 2.0 / tensor_in.shape[-1])
    )
    angles = positions.astype(jnp.float32)[:, None] * frequency[None, :]
    cosine = jnp.cos(angles)[:, None, :]
    sine_part = direction * jnp.sin(angles)[:, None, :]
    first_half = tensor_in[..., :half_dim]
    second_half = tensor_in[..., half_dim:]
    return jnp.concatenate(
        [
            first_half * cosine - second_half * sine_part,
            second_half * cosine + first_half * sine_part,
        ],
        -1,
    )


def allowed_mask(query_pos, query_seg, local_pos, local_seg):
    prompt_pos = jnp.arange(PROMPT, dtype=jnp.int32)
    continued = query_seg[:, None] >= 0
    prompt_part = continued | (prompt_pos[None, :] <= query_pos[:, None])
    local_part = (
        continued
        & (local_seg[None, :] == query_seg[:, None])
        & (local_pos[None, :] <= query_pos[:, None])
    )
    return jnp.concatenate([prompt_part, local_part], 1)


def slot_table(block_routes):
    flat_routes = block_routes.reshape(-1)
    onehot = (flat_routes[:, None] == jnp.arange(EXPERTS, dtype=jnp.int32)[None, :]).astype(
        jnp.int32
    )
    earlier = jnp.cumsum(onehot, 0) - onehot
    rank_in = jnp.sum(earlier * onehot, 1)
    slot_index = flat_routes * CAP + rank_in
    pair_token = jnp.arange(flat_routes.shape[0], dtype=jnp.int32) // TOP
    slot_owner = jnp.full((EXPERTS * CAP,), BLOCK, jnp.int32).at[slot_index].set(pair_token)
    return (slot_index, slot_owner)


def normalize(row_data):
    factor = lax.rsqrt(jnp.mean(row_data * row_data, -1, keepdims=True) + EPSILON)
    return (row_data * factor, factor)


def norm_back(gradient, normed, factor, gain_vec):
    scaled = gradient * gain_vec
    return factor * (scaled - normed * jnp.mean(scaled * normed, -1, keepdims=True))


def spread_rows(gradient, dp_count, tensor_count):
    total_rows = gradient.shape[0]
    shaped = gradient.reshape(
        (dp_count, tensor_count, total_rows // (dp_count * tensor_count)) + gradient.shape[1:]
    )
    return jnp.swapaxes(shaped, 0, 1).reshape(gradient.shape)


def silu_back(pre_act, gradient):
    gate_pre = pre_act[:, 0]
    up_pre = pre_act[:, 1]
    sigmoid_val = jax.nn.sigmoid(gate_pre)
    activated = gate_pre * sigmoid_val
    gate_part = gradient * up_pre * sigmoid_val * (1.0 + gate_pre * (1.0 - sigmoid_val))
    return jnp.stack([gate_part, gradient * activated], 1)


def local(
    inputs,
    cotangent,
    routes,
    gain_attn,
    w_qkv,
    qkv_bias,
    w_out,
    gain_ffn,
    router,
    shared_gate,
    expert_gate_up,
    expert_down,
    shared_gate_up,
    shared_down,
):
    tok_rows = inputs.shape[0]
    model_width = inputs.shape[1]
    dp_count = lax.axis_size("dp")
    tensor_count = lax.axis_size("tensor")
    row_start = lax.axis_index("tensor") * tok_rows
    half_index = lax.axis_index("dp") % 2
    positions, segment = block_layout(half_index)
    half_len = PROMPT // 2
    own_first = half_index == 0
    qkv_full, out_full, bias_full, shared_up_full, shared_down_full = (
        lax.all_gather(w_qkv.astype(jnp.bfloat16), "dp", axis=0, tiled=True),
        lax.all_gather(w_out.astype(jnp.bfloat16), "dp", axis=0, tiled=True),
        lax.all_gather(qkv_bias.astype(jnp.bfloat16), "dp", axis=2, tiled=True),
        lax.all_gather(shared_gate_up.astype(jnp.bfloat16), "dp", axis=0, tiled=True),
        lax.all_gather(shared_down.astype(jnp.bfloat16), "dp", axis=0, tiled=True),
    )
    heads_local = bias_full.shape[1]
    head_width = bias_full.shape[2]
    local_width = heads_local * head_width
    block_in = lax.all_gather(inputs, "tensor", axis=0, tiled=True)
    normed_first, factor_first = normalize(block_in.astype(jnp.float32))
    first_in = (normed_first * gain_attn).astype(jnp.bfloat16)
    projected = jnp.einsum("td,djh->tjh", first_in, qkv_full, preferred_element_type=jnp.float32)
    projected = projected + bias_full.astype(jnp.float32).reshape(3, local_width)
    queries = rotary(
        projected[:, 0].reshape(BLOCK, heads_local, head_width), positions, 1.0
    ).astype(jnp.bfloat16)
    key_block = rotary(
        projected[:, 1].reshape(BLOCK, heads_local, head_width), positions, 1.0
    ).astype(jnp.bfloat16)
    values = projected[:, 2].reshape(BLOCK, heads_local, head_width).astype(jnp.bfloat16)
    partner_keys, partner_values = from_partner((key_block[:half_len], values[:half_len]), "dp", 0)
    prompt_keys = jnp.where(
        own_first,
        jnp.concatenate([key_block[:half_len], partner_keys], 0),
        jnp.concatenate([partner_keys, key_block[:half_len]], 0),
    )
    prompt_values = jnp.where(
        own_first,
        jnp.concatenate([values[:half_len], partner_values], 0),
        jnp.concatenate([partner_values, values[:half_len]], 0),
    )
    scale_factor = head_width ** (-0.5)
    block_count = BLOCK // QBLOCK
    starts = jnp.arange(block_count, dtype=jnp.int32) * QBLOCK

    def block_scores(first_row):
        query_rows = lax.dynamic_slice_in_dim(queries, first_row, QBLOCK, 0)
        key_all = jnp.concatenate(
            [prompt_keys, lax.dynamic_slice_in_dim(key_block, first_row, QBLOCK, 0)], 0
        )
        value_all = jnp.concatenate(
            [prompt_values, lax.dynamic_slice_in_dim(values, first_row, QBLOCK, 0)], 0
        )
        query_pos = lax.dynamic_slice_in_dim(positions, first_row, QBLOCK, 0)
        query_seg = lax.dynamic_slice_in_dim(segment, first_row, QBLOCK, 0)
        allowed = allowed_mask(query_pos, query_seg, query_pos, query_seg)
        scores = (
            jnp.einsum("qhd,khd->hqk", query_rows, key_all, preferred_element_type=jnp.float32)
            * scale_factor
        )
        scores = jnp.where(allowed[None], scores, MASKED)
        return (scores, query_rows, key_all, value_all)

    def attend_block(first_row):
        scores, query_rows, key_all, value_all = block_scores(first_row)
        highest = jnp.max(scores, -1, keepdims=True)
        weights = jnp.exp(scores - highest)
        totals = jnp.sum(weights, -1, keepdims=True)
        attn_probs = (weights / totals).astype(jnp.bfloat16)
        attended = jnp.einsum(
            "hqk,khd->qhd", attn_probs, value_all, preferred_element_type=jnp.float32
        )
        return (attended, (highest + jnp.log(totals))[..., 0])

    attended, log_totals = lax.map(attend_block, starts)
    attended_b = attended.reshape(BLOCK, local_width).astype(jnp.bfloat16)
    attn_local = lax.psum_scatter(
        jnp.einsum("th,dh->td", attended_b, out_full, preferred_element_type=jnp.float32),
        "tensor",
        scatter_dimension=0,
        tiled=True,
    )
    middle = inputs.astype(jnp.float32) + attn_local
    normed_second, factor_second = normalize(middle)
    second_local = (normed_second * gain_ffn).astype(jnp.bfloat16)
    second_in = lax.all_gather(second_local, "tensor", axis=0, tiled=True)
    router_b = router.astype(jnp.bfloat16)
    router_probs = jax.nn.softmax(
        jnp.einsum("td,ed->te", second_in, router_b, preferred_element_type=jnp.float32), -1
    )
    route_onehot = (
        routes[:, :, None] == jnp.arange(EXPERTS, dtype=jnp.int32)[None, None, :]
    ).astype(jnp.float32)
    gate_values = jnp.sum(route_onehot * router_probs[:, None, :], -1).astype(jnp.bfloat16)
    shared_gate_b = shared_gate.astype(jnp.bfloat16)
    shared_prob = jax.nn.sigmoid(
        jnp.dot(second_in, shared_gate_b, preferred_element_type=jnp.float32)
    )
    shared_scale = shared_prob.astype(jnp.bfloat16)
    slot_index, slot_owner = slot_table(routes)
    slot_gate = (
        jnp.zeros((EXPERTS * CAP,), jnp.float32)
        .at[slot_index]
        .set(gate_values.reshape(-1).astype(jnp.float32))
    )
    owner_grid = slot_owner.reshape(EXPERTS, CAP)
    gate_grid = slot_gate.reshape(EXPERTS, CAP)
    padded_in = jnp.concatenate([second_in, jnp.zeros((1, model_width), jnp.bfloat16)], 0)

    def fetch_expert(expert_index):
        gate_up = lax.dynamic_index_in_dim(expert_gate_up, expert_index, 0, keepdims=False).astype(
            jnp.bfloat16
        )
        down_rows = lax.dynamic_index_in_dim(expert_down, expert_index, 0, keepdims=False).astype(
            jnp.bfloat16
        )
        return (
            lax.all_gather(gate_up, "dp", axis=2, tiled=True),
            lax.all_gather(down_rows, "dp", axis=1, tiled=True),
        )

    def expert_forward(combined, expert_index):
        gate_up, down_rows = fetch_expert(expert_index)
        takers = owner_grid[expert_index]
        taken = padded_in[takers]
        pre_act = jnp.einsum("cd,jfd->cjf", taken, gate_up, preferred_element_type=jnp.float32)
        hidden = (jax.nn.silu(pre_act[:, 0]) * pre_act[:, 1]).astype(jnp.bfloat16)
        result = jnp.einsum("cf,fd->cd", hidden, down_rows, preferred_element_type=jnp.float32)
        combined = combined.at[takers].add(result * gate_grid[expert_index][:, None])
        stored = (pre_act,)
        return (combined, stored)

    expert_ids = jnp.arange(EXPERTS, dtype=jnp.int32)
    combined, stored = lax.scan(
        expert_forward, jnp.zeros((BLOCK + 1, model_width), jnp.float32), expert_ids
    )
    shared_pre = jnp.einsum(
        "td,djf->tjf", second_in, shared_up_full, preferred_element_type=jnp.float32
    )
    shared_hidden = (jax.nn.silu(shared_pre[:, 0]) * shared_pre[:, 1]).astype(jnp.bfloat16)
    shared_result = jnp.einsum(
        "tf,df->td", shared_hidden, shared_down_full, preferred_element_type=jnp.float32
    )
    mixed_part = combined[:BLOCK] + shared_scale.astype(jnp.float32)[:, None] * shared_result
    mixed_local = lax.psum_scatter(
        mixed_part.astype(jnp.bfloat16), "tensor", scatter_dimension=0, tiled=True
    ).astype(jnp.float32)
    layer_out = (middle + mixed_local).astype(jnp.bfloat16)
    grad_rows = lax.all_gather(cotangent, "tensor", axis=0, tiled=True)
    padded_grad = jnp.concatenate([grad_rows, jnp.zeros((1, model_width), jnp.bfloat16)], 0)

    def expert_backward(running, scanned):
        grad_second, slot_grad = running
        expert_index = scanned[0]
        pre_act = scanned[1]
        gate_up, down_rows = fetch_expert(expert_index)
        takers = owner_grid[expert_index]
        taken = padded_in[takers]
        taken_grad = padded_grad[takers].astype(jnp.float32)
        hidden = (jax.nn.silu(pre_act[:, 0]) * pre_act[:, 1]).astype(jnp.bfloat16)
        result = jnp.einsum("cf,fd->cd", hidden, down_rows, preferred_element_type=jnp.float32)
        slot_grad = slot_grad.at[expert_index].set(jnp.sum(taken_grad * result, -1))
        result_grad = (gate_grid[expert_index][:, None] * taken_grad).astype(jnp.bfloat16)
        hidden_grad = jnp.einsum(
            "cd,fd->cf", result_grad, down_rows, preferred_element_type=jnp.float32
        )
        pre_grad = silu_back(pre_act, hidden_grad).astype(jnp.bfloat16)
        rows_back = jnp.einsum("cjf,jfd->cd", pre_grad, gate_up, preferred_element_type=jnp.float32)
        grad_second = grad_second.at[takers].add(rows_back)
        first_part = jnp.einsum("cd,cjf->djf", taken, pre_grad, preferred_element_type=jnp.float32)
        second_part = jnp.einsum(
            "cd,cf->df", result_grad, hidden, preferred_element_type=jnp.float32
        )
        weight_grad = lax.psum_scatter(
            jnp.concatenate([first_part, second_part[:, None]], 1).astype(jnp.bfloat16),
            "dp",
            scatter_dimension=0,
            tiled=True,
        ).astype(jnp.float32)
        return ((grad_second, slot_grad), weight_grad)

    start_state = (
        jnp.zeros((BLOCK + 1, model_width), jnp.float32),
        jnp.zeros((EXPERTS, CAP), jnp.float32),
    )
    (grad_second, slot_grad), weight_grads = lax.scan(
        expert_backward, start_state, (expert_ids,) + stored
    )
    expert_gate_up_grad = jnp.transpose(weight_grads[:, :, :2], (0, 2, 3, 1))
    expert_down_grad = jnp.transpose(weight_grads[:, :, 2], (0, 2, 1))
    gate_grad = slot_grad.reshape(-1)[slot_index].reshape(BLOCK, TOP)
    prob_grad = jnp.sum(route_onehot * gate_grad[:, :, None], 1)
    logit_grad = router_probs * (prob_grad - jnp.sum(router_probs * prob_grad, -1, keepdims=True))
    router_part = jnp.einsum(
        "td,te->de", second_in, logit_grad, precision=HIGHEST, preferred_element_type=jnp.float32
    )
    grad_second = grad_second[:BLOCK] + jnp.dot(
        logit_grad, router_b.astype(jnp.float32), precision=HIGHEST
    )
    grad_rows_f = grad_rows.astype(jnp.float32)
    shared_scale_grad = jnp.sum(grad_rows_f * shared_result, -1)
    shared_result_grad = (shared_scale.astype(jnp.float32)[:, None] * grad_rows_f).astype(
        jnp.bfloat16
    )
    shared_hidden_grad = jnp.einsum(
        "td,df->tf", shared_result_grad, shared_down_full, preferred_element_type=jnp.float32
    )
    shared_pre_grad = silu_back(shared_pre, shared_hidden_grad).astype(jnp.bfloat16)
    shared_down_part = jnp.einsum(
        "td,tf->df", shared_result_grad, shared_hidden, preferred_element_type=jnp.float32
    )
    shared_up_part = jnp.einsum(
        "td,tjf->djf", second_in, shared_pre_grad, preferred_element_type=jnp.float32
    )
    grad_second = grad_second + jnp.einsum(
        "tjf,djf->td", shared_pre_grad, shared_up_full, preferred_element_type=jnp.float32
    )
    shared_logit_grad = shared_scale_grad * shared_prob * (1.0 - shared_prob)
    shared_gate_part = jnp.einsum(
        "td,t->d",
        second_in,
        shared_logit_grad,
        precision=HIGHEST,
        preferred_element_type=jnp.float32,
    )
    grad_second = (
        grad_second + shared_logit_grad[:, None] * shared_gate_b.astype(jnp.float32)[None, :]
    )
    router_spread = jnp.transpose(spread_rows(router_part, dp_count, tensor_count))
    second_grad, router_share, shared_gate_share = (
        lax.psum_scatter(grad_second, "tensor", scatter_dimension=0, tiled=True),
        lax.psum_scatter(router_spread, "tensor", scatter_dimension=1, tiled=True),
        lax.psum_scatter(
            spread_rows(shared_gate_part, dp_count, tensor_count),
            "tensor",
            scatter_dimension=0,
            tiled=True,
        ),
    )
    gain_ffn_part = jnp.sum(second_grad * normed_second, 0)
    middle_grad = cotangent.astype(jnp.float32) + norm_back(
        second_grad, normed_second, factor_second, gain_ffn
    )
    branch_grad = lax.all_gather(middle_grad.astype(jnp.bfloat16), "tensor", axis=0, tiled=True)
    attended_grad = jnp.einsum(
        "td,dh->th", branch_grad, out_full, preferred_element_type=jnp.float32
    ).astype(jnp.bfloat16)
    w_out_part = jnp.einsum(
        "td,th->dh", branch_grad, attended_b, preferred_element_type=jnp.float32
    )
    attended_grad = attended_grad.reshape(block_count, QBLOCK, heads_local, head_width)

    def attend_back(running, scanned):
        key_sums, value_sums = running
        first_row, log_total, out_grad = scanned
        scores, query_rows, key_all, value_all = block_scores(first_row)
        attn_probs = jnp.exp(scores - log_total[..., None])
        probs_b = attn_probs.astype(jnp.bfloat16)
        attn_prob_grad = jnp.einsum(
            "qhd,khd->hqk", out_grad, value_all, preferred_element_type=jnp.float32
        )
        score_grad = attn_probs * (
            attn_prob_grad - jnp.sum(attn_probs * attn_prob_grad, -1, keepdims=True)
        )
        score_grad = score_grad.astype(jnp.bfloat16)
        query_grad = (
            jnp.einsum("hqk,khd->qhd", score_grad, key_all, preferred_element_type=jnp.float32)
            * scale_factor
        )
        key_grad = (
            jnp.einsum("hqk,qhd->khd", score_grad, query_rows, preferred_element_type=jnp.float32)
            * scale_factor
        )
        value_grad = jnp.einsum(
            "hqk,qhd->khd", probs_b, out_grad, preferred_element_type=jnp.float32
        )
        running = (key_sums + key_grad[:PROMPT], value_sums + value_grad[:PROMPT])
        return (running, (query_grad, key_grad[PROMPT:], value_grad[PROMPT:]))

    empty_prompt = jnp.zeros((PROMPT, heads_local, head_width), jnp.float32)
    (key_sums, value_sums), (query_grads, local_key_grads, local_value_grads) = lax.scan(
        attend_back, (empty_prompt, empty_prompt), (starts, log_totals, attended_grad)
    )
    own_keys = jnp.where(own_first, key_sums[:half_len], key_sums[half_len:])
    other_keys = jnp.where(own_first, key_sums[half_len:], key_sums[:half_len])
    own_values = jnp.where(own_first, value_sums[:half_len], value_sums[half_len:])
    other_values = jnp.where(own_first, value_sums[half_len:], value_sums[:half_len])
    back_keys, back_values = (
        from_partner(other_keys.astype(jnp.bfloat16), "dp", 0).astype(other_keys.dtype),
        from_partner(other_values.astype(jnp.bfloat16), "dp", 0).astype(other_values.dtype),
    )
    key_grad_rows = local_key_grads.reshape(BLOCK, heads_local, head_width)
    key_grad_rows = jnp.concatenate(
        [key_grad_rows[:half_len] + own_keys + back_keys, key_grad_rows[half_len:]], 0
    )
    value_grad_rows = local_value_grads.reshape(BLOCK, heads_local, head_width)
    value_grad_rows = jnp.concatenate(
        [value_grad_rows[:half_len] + own_values + back_values, value_grad_rows[half_len:]], 0
    )
    query_grad_rows = query_grads.reshape(BLOCK, heads_local, head_width)
    qkv_grad = (
        jnp.stack(
            [
                rotary(query_grad_rows, positions, -1.0),
                rotary(key_grad_rows, positions, -1.0),
                value_grad_rows,
            ],
            1,
        )
        .reshape(BLOCK, 3, local_width)
        .astype(jnp.bfloat16)
    )
    bias_part = jnp.sum(qkv_grad.astype(jnp.float32), 0).reshape(3, heads_local, head_width)
    w_qkv_part = jnp.einsum("td,tjh->djh", first_in, qkv_grad, preferred_element_type=jnp.float32)
    first_grad_part = jnp.einsum(
        "tjh,djh->td", qkv_grad, qkv_full, preferred_element_type=jnp.float32
    )
    gain_attn_part = jnp.sum(first_grad_part * normed_first, 0)
    first_grad, gain_attn_share, gain_ffn_share = (
        lax.psum_scatter(
            first_grad_part.astype(jnp.bfloat16), "tensor", scatter_dimension=0, tiled=True
        ).astype(jnp.float32),
        lax.psum_scatter(
            spread_rows(gain_attn_part, dp_count, tensor_count).astype(jnp.bfloat16),
            "tensor",
            scatter_dimension=0,
            tiled=True,
        ).astype(jnp.float32),
        lax.psum_scatter(
            spread_rows(gain_ffn_part, dp_count, tensor_count).astype(jnp.bfloat16),
            "tensor",
            scatter_dimension=0,
            tiled=True,
        ).astype(jnp.float32),
    )
    normed_local = lax.dynamic_slice_in_dim(normed_first, row_start, tok_rows, 0)
    factor_local = lax.dynamic_slice_in_dim(factor_first, row_start, tok_rows, 0)
    input_grad = middle_grad + norm_back(first_grad, normed_local, factor_local, gain_attn)
    summed = (
        lax.psum_scatter(
            w_qkv_part.astype(jnp.bfloat16), "dp", scatter_dimension=0, tiled=True
        ).astype(jnp.float32),
        lax.psum_scatter(
            w_out_part.astype(jnp.bfloat16), "dp", scatter_dimension=0, tiled=True
        ).astype(jnp.float32),
        lax.psum_scatter(
            bias_part.astype(jnp.bfloat16), "dp", scatter_dimension=2, tiled=True
        ).astype(jnp.float32),
        lax.psum_scatter(
            shared_up_part.astype(jnp.bfloat16), "dp", scatter_dimension=0, tiled=True
        ).astype(jnp.float32),
        lax.psum_scatter(
            shared_down_part.astype(jnp.bfloat16), "dp", scatter_dimension=0, tiled=True
        ).astype(jnp.float32),
        lax.psum_scatter(
            gain_attn_share.astype(jnp.bfloat16), "dp", scatter_dimension=0, tiled=True
        ).astype(jnp.float32),
        lax.psum_scatter(
            gain_ffn_share.astype(jnp.bfloat16), "dp", scatter_dimension=0, tiled=True
        ).astype(jnp.float32),
        lax.psum_scatter(
            router_share.astype(jnp.bfloat16), "dp", scatter_dimension=1, tiled=True
        ).astype(jnp.float32),
        lax.psum_scatter(
            shared_gate_share.astype(jnp.bfloat16), "dp", scatter_dimension=0, tiled=True
        ).astype(jnp.float32),
    )
    return (
        layer_out,
        input_grad,
        summed[5],
        summed[0],
        summed[2],
        summed[1],
        summed[6],
        summed[7],
        summed[8],
        expert_gate_up_grad,
        expert_down_grad,
        summed[3],
        summed[4],
    )


def solution(mesh):
    return jax.shard_map(
        local,
        mesh=mesh,
        in_specs=(
            P(("dp", "tensor"), None),
            P(("dp", "tensor"), None),
            P("dp", None),
            P(),
            P("dp", None, "tensor"),
            P(None, "tensor", "dp"),
            P("dp", "tensor"),
            P(),
            P(),
            P(),
            P(None, None, "tensor", "dp"),
            P(None, "tensor", "dp"),
            P("dp", None, "tensor"),
            P("dp", "tensor"),
        ),
        out_specs=(
            P(("dp", "tensor"), None),
            P(("dp", "tensor"), None),
            P(("dp", "tensor")),
            P("dp", None, "tensor"),
            P(None, "tensor", "dp"),
            P("dp", "tensor"),
            P(("dp", "tensor")),
            P(None, ("dp", "tensor")),
            P(("dp", "tensor")),
            P(None, None, "tensor", "dp"),
            P(None, "tensor", "dp"),
            P("dp", None, "tensor"),
            P("dp", "tensor"),
        ),
        check_vma=False,
    )
```

profile of v0, /device:TPU:0, one launch (start us, length us, event | category | flops | bytes accessed | tf_op | source)
XLA Modules:
  0.0 5093.9 jit_solution(11559327569503071163)
XLA Ops:
  31.2 51.4 %all-gather.25.cloned.1.call-done = bf16[1536,2048]{1,0:T(8,128)(2,1)} async-done(((bf16[384,2048]{1,0:T(8,128)(2,1)}), bf16[1536,2048]{1,0:T(8,128)(2,1)}) %all-gather.25.cloned.1.call-update) | async-done | bytes 6291472 | tf_op jit(solution)/shard_map/all_gather | solution.py:144
  86.7 63.2 %all-gather.27.cloned.1.call-done = bf16[2048,3,512]{0,2,1:T(8,128)(2,1)} async-done(((bf16[256,3,512]{0,2,1:T(8,128)(2,1)}), bf16[2048,3,512]{0,2,1:T(8,128)(2,1)}) %all-gather.27.cloned.1.call-update) | async-done | bytes 6291472 | tf_op jit(solution)/shard_map/all_gather | solution.py:135
  212.8 106.2 %while.58 = (s32[]{:T(128)}, bf16[3,512,4,128]{1,3,2,0:T(8,128)(2,1)}, f32[3,4,512]{2,1,0:T(4,128)}, s32[3]{0:T(128)S(1)}, bf16[1536,4,128]{0,2,1:T(8,128)(2,1)}...) while((s32[]{:T(128)}, ...), condition=%wide.region_4.5_spmd, body=%wide.region_1.4_spmd.sunk | while | flops 2762209792 | bytes 163660512 | solution.py:200
  331.2 118.2 %reduce-scatter.17.cloned.1.call-done = f32[384,2048]{1,0:T(8,128)} async-done(((f32[1536,2048]{1,0:T(8,128)}), f32[384,2048]{1,0:T(8,128)}) %reduce-scatter.17.cloned.1.call-update) | async-done | bytes 3145744 | tf_op jit(solution)/shard_map/reduce_scatter | solution.py:202
  527.7 65.8 %all-gather.31.cloned.1.call-done = bf16[1536,2048]{1,0:T(8,128)(2,1)} async-done(((bf16[384,2048]{1,0:T(8,128)(2,1)}), bf16[1536,2048]{1,0:T(8,128)(2,1)}) %all-gather.31.cloned.1.call-update) | async-done | bytes 6291472 | tf_op jit(solution)/shard_map/all_gather | solution.py:211
  636.0 1354.8 %while.59 = (s32[]{:T(128)}, f32[1537,2048]{1,0:T(8,128)}, f32[16,408,2,352]{3,1,2,0:T(8,128)}, s32[16]{0:T(128)S(1)}, s32[16,408]{1,0:T(8,128)S(1)}, /*index=5*...) while((s32[]{:T(128)}, f32[1537,2048]{1,0:T(8,128)}, ...), condition=%wide.region_17.18_spmd, body=%wide.region_15.17_spmd.sunk | while | flops 1767288576 | bytes 47966032 | solution.py:259
  1996.9 1932.2 %while.60 = (s32[]{:T(128)}, f32[1537,2048]{1,0:T(8,128)}, f32[16,408]{1,0:T(8,128)S(1)}, f32[16,256,3,352]{1,3,2,0:T(8,128)}, s32[16]{0:T(128)S(1)}, /*index=5*...) while((s32[]{:T(128)}, f32[1537,2048]{1,0:T(8,128)}, ...), condition=%wide.region_24.25_spmd, body=%wide.region_19.24_spmd.sunk | while | flops 4134302208 | bytes 98562960 | solution.py:311
  2083.1 32.9 reduce-scatter.39.cloned.1.call-done
  2203.8 32.9 reduce-scatter.39.cloned.1.call-done
  2445.0 32.9 reduce-scatter.39.cloned.1.call-done
  2686.6 32.9 reduce-scatter.39.cloned.1.call-done
  3048.7 32.9 reduce-scatter.39.cloned.1.call-done
  3169.4 32.9 reduce-scatter.39.cloned.1.call-done
  3290.1 32.9 reduce-scatter.39.cloned.1.call-done
  3531.4 32.9 reduce-scatter.39.cloned.1.call-done
  3652.3 32.9 reduce-scatter.39.cloned.1.call-done
  3773.0 32.9 reduce-scatter.39.cloned.1.call-done
  3932.4 34.3 gather_fusion.3
  3972.6 65.8 %all-gather.33.cloned.1.call-done = bf16[2048,2,1408]{2,0,1:T(8,128)(2,1)} async-done(((bf16[256,2,1408]{2,0,1:T(8,128)(2,1)}), bf16[2048,2,1408]{2,0,1:T(8,128)(2,1)}) %all-gather.33.cloned.1.call-update) | async-done | bytes 11534352 | tf_op jit(solution)/shard_map/all_gather | solution.py:138
  4064.2 35.0 all-gather.35.cloned.1.call-done
  4188.5 111.9 %reduce-scatter.21.cloned.1.call-done = f32[384,2048]{1,0:T(8,128)} async-done(((f32[1536,2048]{1,0:T(8,128)}), f32[384,2048]{1,0:T(8,128)}) %reduce-scatter.21.cloned.1.call-update) | async-done | bytes 3145744 | tf_op jit(solution)/shard_map/reduce_scatter | solution.py:356
  4413.2 306.6 %while.61 = (s32[]{:T(128)}, f32[2048,4,128]{0,2,1:T(8,128)}, f32[2048,4,128]{0,2,1:T(8,128)}, f32[3,512,4,128]{3,1,0,2:T(8,128)}, f32[3,512,4,128]{1,3,2,0:T(8,...) while((s32[]{:T(128)}, f32[2048,4,128]{0,2,1:T(8,128)}, ...), condition=%wide.region_32.33_spmd.clone, body=%wide.region_30.32_spmd.clone.sunk | while | flops 6815480320 | bytes 323036096 | solution.py:406
  4938.7 68.9 %reduce-scatter.23.cloned.1.call-done = bf16[384,2048]{1,0:T(8,128)(2,1)} async-done(((bf16[1536,2048]{1,0:T(8,128)(2,1)}), bf16[384,2048]{1,0:T(8,128)(2,1)}) %reduce-scatter.23.cloned.1.call-update) | async-done | bytes 1572880 | tf_op jit(solution)/shard_map/reduce_scatter | solution.py:445
  5010.5 70.0 %reduce-scatter.19.cloned.1.call-done = bf16[384,2048]{1,0:T(8,128)(2,1)} async-done(((bf16[1536,2048]{1,0:T(8,128)(2,1)}), bf16[384,2048]{1,0:T(8,128)(2,1)}) %reduce-scatter.19.cloned.1.call-update) | async-done | bytes 1572880 | tf_op jit(solution)/shard_map/reduce_scatter | solution.py:270
  (1356 shorter events, 3983.6 us)
Async XLA Ops:
  7.9 142.0 %all-gather.27.cloned.1.call-start = ((), (), s32[]{:S(2)}) async-start(), calls=%async_computation.13 | async-start | bytes 7077888 | tf_op jit(solution)/shard_map/all_gather | solution.py:135
  10.6 311.2 %all-gather.29.cloned.1.call-start = ((), (), s32[]{:S(2)}) async-start(), calls=%async_computation.14 | async-start | bytes 2359296 | tf_op jit(solution)/shard_map/all_gather | solution.py:136
  194.9 254.5 %reduce-scatter.17.cloned.1.call-start = ((), (), s32[]{:S(2)}) async-start(), calls=%async_computation.15 | async-start | bytes 15728640 | tf_op jit(solution)/shard_map/reduce_scatter | solution.py:202
  330.4 190.8 %all-gather.37.cloned.1.call-start = ((), (), s32[]{:S(2)}) async-start(), calls=%async_computation.20 | async-start | bytes 7864320 | tf_op jit(solution)/shard_map/all_gather | solution.py:274
  331.0 262.5 %all-gather.31.cloned.1.call-start = ((), (), s32[]{:S(2)}) async-start(), calls=%async_computation.16 | async-start | bytes 7864320 | tf_op jit(solution)/shard_map/all_gather | solution.py:211
  2003.2 112.8 %reduce-scatter.39.cloned.1.call-start = ((), (), s32[]{:S(2)}) async-start(), calls=%async_computation.35 | async-start | bytes 4866048 | tf_op jit(solution)/shard_map/while/body/eval_jaxpr/reduce_scatter | solution.py:299
  2486.1 112.6 %reduce-scatter.39.cloned.1.call-start = ((), (), s32[]{:S(2)}) async-start(), calls=%async_computation.35 | async-start | bytes 4866048 | tf_op jit(solution)/shard_map/while/body/eval_jaxpr/reduce_scatter | solution.py:299
  2606.8 112.7 %reduce-scatter.39.cloned.1.call-start = ((), (), s32[]{:S(2)}) async-start(), calls=%async_computation.35 | async-start | bytes 4866048 | tf_op jit(solution)/shard_map/while/body/eval_jaxpr/reduce_scatter | solution.py:299
  2848.2 112.7 %reduce-scatter.39.cloned.1.call-start = ((), (), s32[]{:S(2)}) async-start(), calls=%async_computation.35 | async-start | bytes 4866048 | tf_op jit(solution)/shard_map/while/body/eval_jaxpr/reduce_scatter | solution.py:299
  2969.1 112.6 %reduce-scatter.39.cloned.1.call-start = ((), (), s32[]{:S(2)}) async-start(), calls=%async_computation.35 | async-start | bytes 4866048 | tf_op jit(solution)/shard_map/while/body/eval_jaxpr/reduce_scatter | solution.py:299
  3572.5 112.8 %reduce-scatter.39.cloned.1.call-start = ((), (), s32[]{:S(2)}) async-start(), calls=%async_computation.35 | async-start | bytes 4866048 | tf_op jit(solution)/shard_map/while/body/eval_jaxpr/reduce_scatter | solution.py:299
  3814.1 112.6 %reduce-scatter.39.cloned.1.call-start = ((), (), s32[]{:S(2)}) async-start(), calls=%async_computation.35 | async-start | bytes 4866048 | tf_op jit(solution)/shard_map/while/body/eval_jaxpr/reduce_scatter | solution.py:299
  3929.8 169.3 %all-gather.35.cloned.1.call-start = ((), (), s32[]{:S(2)}) async-start(), calls=%async_computation.18 | async-start | bytes 6488064 | tf_op jit(solution)/shard_map/all_gather | solution.py:139
  3932.2 368.3 %reduce-scatter.21.cloned.1.call-start = ((), (), s32[]{:S(2)}) async-start(), calls=%async_computation.21 | async-start | bytes 15728640 | tf_op jit(solution)/shard_map/reduce_scatter | solution.py:356
  4181.0 146.9 %reduce-scatter.29.cloned.1.call-start = ((), (), s32[]{:S(2)}) async-start(), calls=%async_computation.26 | async-start | bytes 163840 | tf_op jit(solution)/shard_map/reduce_scatter | solution.py:357
  4188.5 212.0 %all-gather.39.cloned.1.call-start = ((), (), s32[]{:S(2)}) async-start(), calls=%async_computation.22 | async-start | bytes 7864320 | tf_op jit(solution)/shard_map/all_gather | solution.py:369
  4306.0 565.8 %reduce-scatter.37.cloned.1.call-start = ((), (), s32[]{:S(2)}) async-start(), calls=%async_computation.30 | async-start | bytes 147456
  4329.5 543.8 %reduce-scatter.33.cloned.1.call-start = ((), (), s32[]{:S(2)}) async-start(), calls=%async_computation.28 | async-start | bytes 6488064 | tf_op jit(solution)/shard_map/reduce_scatter | solution.py:477
  4345.2 530.4 %reduce-scatter.31.cloned.1.call-start = ((), (), s32[]{:S(2)}) async-start(), calls=%async_computation.27 | async-start | bytes 12976128 | tf_op jit(solution)/shard_map/reduce_scatter | solution.py:474
  4369.7 548.5 %reduce-scatter.35.cloned.1.call-start = ((), (), s32[]{:S(2)}) async-start(), calls=%async_computation.29 | async-start | bytes 36864
  4797.3 122.4 %reduce-scatter.27.cloned.1.call-start = ((), (), s32[]{:S(2)}) async-start(), calls=%async_computation.25 | async-start | bytes 2359296 | tf_op jit(solution)/shard_map/reduce_scatter | solution.py:468
  4805.4 130.8 %reduce-scatter.25.cloned.1.call-start = ((), (), s32[]{:S(2)}) async-start(), calls=%async_computation.24 | async-start | bytes 7077888 | tf_op jit(solution)/shard_map/reduce_scatter | solution.py:465
  4822.1 185.5 %reduce-scatter.23.cloned.1.call-start = ((), (), s32[]{:S(2)}) async-start(), calls=%async_computation.23 | async-start | bytes 7864320 | tf_op jit(solution)/shard_map/reduce_scatter | solution.py:445
  4838.5 242.0 %reduce-scatter.19.cloned.1.call-start = ((), (), s32[]{:S(2)}) async-start(), calls=%async_computation.19 | async-start | bytes 7864320 | tf_op jit(solution)/shard_map/reduce_scatter | solution.py:270
  (235 other events, 7101.1 us)
Sparse Core Ops, SparseCore 0:
  9.8 72.7 all-gather.24
  84.8 65.1 all-gather.26
  330.5 118.8 reduce-scatter.16
  451.1 70.0 all-gather.36
  523.5 70.0 all-gather.30
  2187.3 49.3 reduce-scatter.38
  2307.9 49.3 reduce-scatter.38
  2549.3 49.3 reduce-scatter.38
  2670.2 49.3 reduce-scatter.38
  2790.7 49.3 reduce-scatter.38
  3153.0 49.3 reduce-scatter.38
  3273.7 49.3 reduce-scatter.38
  3515.0 49.3 reduce-scatter.38
  3756.5 49.3 reduce-scatter.38
  3877.3 49.3 reduce-scatter.38
  3931.9 106.4 all-gather.32
  4040.5 58.6 all-gather.34
  4181.1 119.2 reduce-scatter.20
  4330.4 70.0 all-gather.38
  4435.3 62.8 reduce-scatter.32
  4500.6 117.6 reduce-scatter.30
  4867.5 68.6 reduce-scatter.24
  4939.1 68.4 reduce-scatter.22
  5010.4 70.0 reduce-scatter.18
  (75 shorter events, 2372.5 us)
where the time goes:
time: 5120 us; the launch traced here: 5090 us
  waiting for transfers between devices  2520 us (49%)
  local copies, waits for them, and re-layouts  868 us (17%)
  other arithmetic  808 us (16%)
  matrix products  752 us (15%)
  loops' own time  79.6 us (2%)
    all_gather x32, waiting for transfers between devices, fetch_expert(): lax.all_gather(gate_up, 'dp', axis=2, tiled=True)  819 us
    reduce_scatter x16, waiting for transfers between devices, expert_backward(): lax.psum_scatter(jnp.concatenate([first_part, second_part[:, None]], 1).a...  526 us
    all_gather x32, waiting for transfers between devices, fetch_expert(): lax.all_gather(down_rows, 'dp', axis=1, tiled=True)  426 us
    scatter-add x16, other arithmetic, expert_backward(): grad_second = grad_second.at[takers].add(rows_back)  244 us
    scatter-add x16, other arithmetic, expert_forward(): combined.at[takers].add(result * gate_grid[expert_index][:, None])  239 us
    gather x16, local copies, waits for them, and re-layouts, expert_backward(): taken = padded_in[takers]  128 us
    gather x16, local copies, waits for them, and re-layouts, expert_forward(): taken = padded_in[takers]  128 us
    gather x16, local copies, waits for them, and re-layouts, expert_backward(): taken_grad = padded_grad[takers].astype(jnp.float32)  128 us
  transfers between devices with their start and end apart: 103, of which 93 were waited for; matrix products, arithmetic and copies ran while one was open for 36% of the time, Pallas kernels for 0%

commit v1 on v0

--- a/solution.py
+++ b/solution.py
@@ -16,7 +16,6 @@
 EPSILON = 1e-06
 ROPE_BASE = 1000000.0
 MASKED = -1000000000.0
-HIGHEST = lax.Precision.HIGHEST
 
 
 def from_partner(value, axis, distance):
@@ -66,17 +65,80 @@
     return jnp.concatenate([prompt_part, local_part], 1)
 
 
-def slot_table(block_routes):
-    flat_routes = block_routes.reshape(-1)
-    onehot = (flat_routes[:, None] == jnp.arange(EXPERTS, dtype=jnp.int32)[None, :]).astype(
-        jnp.int32
-    )
-    earlier = jnp.cumsum(onehot, 0) - onehot
-    rank_in = jnp.sum(earlier * onehot, 1)
-    slot_index = flat_routes * CAP + rank_in
-    pair_token = jnp.arange(flat_routes.shape[0], dtype=jnp.int32) // TOP
-    slot_owner = jnp.full((EXPERTS * CAP,), BLOCK, jnp.int32).at[slot_index].set(pair_token)
-    return (slot_index, slot_owner)
+def expert_groups(dp_count, tensor_count):
+    blocks = EXPERTS // tensor_count
+    replicas = dp_count // blocks
+    members = [
+        [
+            (i * replicas + g) * tensor_count + t
+            for i in range(blocks)
+            for t in range(tensor_count)
+        ]
+        for g in range(replicas)
+    ]
+    return (blocks, replicas, members)
+
+
+def swap_groups(value, members):
+    return lax.all_to_all(
+        value, ("dp", "tensor"), split_axis=0, concat_axis=0, tiled=True, axis_index_groups=members
+    )
+
+
+def sum_over_tensor(value):
+    count = lax.axis_size("tensor")
+    pieces = lax.all_to_all(value, "tensor", split_axis=0, concat_axis=0, tiled=True)
+    pieces = pieces.reshape((count, value.shape[0] // count) + value.shape[1:])
+    return jnp.sum(pieces.astype(jnp.float32), 0)
+
+
+def gather_expert(gate_up, down_rows, groups):
+    blocks, replicas, members = groups
+    dp_count = lax.axis_size("dp")
+    tensor_count = lax.axis_size("tensor")
+    hidden_part = down_rows.shape[1]
+    width_part = down_rows.shape[2]
+    packed = jnp.concatenate(
+        [gate_up.astype(jnp.bfloat16), down_rows.astype(jnp.bfloat16)[:, None]], 1
+    ).reshape(EXPERTS, 3 * hidden_part, width_part)
+    own = swap_groups(packed, members)
+    if replicas == 2:
+        other = lax.ppermute(own, "dp", [(s, s ^ 1) for s in range(dp_count)])
+        first = lax.axis_index("dp") % 2 == 0
+        both = jnp.stack([jnp.where(first, own, other), jnp.where(first, other, own)])
+    else:
+        lines = [[i * replicas + g for g in range(replicas)] for i in range(blocks)]
+        both = lax.all_gather(own, "dp", axis=0, tiled=False, axis_index_groups=lines)
+    both = both.reshape(replicas, blocks, tensor_count, 3, hidden_part, width_part)
+    both = jnp.transpose(both, (3, 2, 4, 1, 0, 5))
+    return both.reshape(3, tensor_count * hidden_part, dp_count * width_part)
+
+
+def return_expert_grads(grads, groups):
+    blocks, replicas, members = groups
+    dp_count = lax.axis_size("dp")
+    tensor_count = lax.axis_size("tensor")
+    hidden_part = grads.shape[1] // tensor_count
+    width_part = grads.shape[2] // dp_count
+    split = grads.reshape(3, tensor_count, hidden_part, blocks, replicas, width_part)
+    split = jnp.transpose(split, (4, 3, 1, 0, 2, 5)).reshape(
+        replicas, EXPERTS, 3 * hidden_part, width_part
+    )
+    if replicas == 2:
+        first = lax.axis_index("dp") % 2 == 0
+        own = jnp.where(first, split[0], split[1])
+        other = jnp.where(first, split[1], split[0])
+        back = lax.ppermute(other, "dp", [(s, s ^ 1) for s in range(dp_count)])
+        summed = (own.astype(jnp.float32) + back.astype(jnp.float32)).astype(jnp.bfloat16)
+    else:
+        lines = [[i * replicas + g for g in range(replicas)] for i in range(blocks)]
+        pieces = lax.all_to_all(
+            split, "dp", split_axis=0, concat_axis=0, tiled=True, axis_index_groups=lines
+        )
+        summed = jnp.sum(pieces.astype(jnp.float32), 0).astype(jnp.bfloat16)
+    shares = swap_groups(summed, members).astype(jnp.float32)
+    shares = shares.reshape(EXPERTS, 3, hidden_part, width_part)
+    return (shares[:, :2], shares[:, 2])
 
 
 def normalize(row_data):
@@ -87,14 +149,6 @@
 def norm_back(gradient, normed, factor, gain_vec):
     scaled = gradient * gain_vec
     return factor * (scaled - normed * jnp.mean(scaled * normed, -1, keepdims=True))
-
-
-def spread_rows(gradient, dp_count, tensor_count):
-    total_rows = gradient.shape[0]
-    shaped = gradient.reshape(
-        (dp_count, tensor_count, total_rows // (dp_count * tensor_count)) + gradient.shape[1:]
-    )
-    return jnp.swapaxes(shaped, 0, 1).reshape(gradient.shape)
 
 
 def silu_back(pre_act, gradient):
@@ -127,6 +181,7 @@
     dp_count = lax.axis_size("dp")
     tensor_count = lax.axis_size("tensor")
     row_start = lax.axis_index("tensor") * tok_rows
+    groups = expert_groups(dp_count, tensor_count)
     half_index = lax.axis_index("dp") % 2
     positions, segment = block_layout(half_index)
     half_len = PROMPT // 2
@@ -138,6 +193,7 @@
         lax.all_gather(shared_gate_up.astype(jnp.bfloat16), "dp", axis=0, tiled=True),
         lax.all_gather(shared_down.astype(jnp.bfloat16), "dp", axis=0, tiled=True),
     )
+    expert_rows = gather_expert(expert_gate_up, expert_down, groups)
     heads_local = bias_full.shape[1]
     head_width = bias_full.shape[2]
     local_width = heads_local * head_width
@@ -199,66 +255,74 @@
 
     attended, log_totals = lax.map(attend_block, starts)
     attended_b = attended.reshape(BLOCK, local_width).astype(jnp.bfloat16)
-    attn_local = lax.psum_scatter(
-        jnp.einsum("th,dh->td", attended_b, out_full, preferred_element_type=jnp.float32),
-        "tensor",
-        scatter_dimension=0,
-        tiled=True,
+    attn_local = sum_over_tensor(
+        jnp.einsum("th,dh->td", attended_b, out_full, preferred_element_type=jnp.float32).astype(
+            jnp.bfloat16
+        )
     )
     middle = inputs.astype(jnp.float32) + attn_local
     normed_second, factor_second = normalize(middle)
     second_local = (normed_second * gain_ffn).astype(jnp.bfloat16)
     second_in = lax.all_gather(second_local, "tensor", axis=0, tiled=True)
-    router_b = router.astype(jnp.bfloat16)
-    router_probs = jax.nn.softmax(
-        jnp.einsum("td,ed->te", second_in, router_b, preferred_element_type=jnp.float32), -1
-    )
-    route_onehot = (
-        routes[:, :, None] == jnp.arange(EXPERTS, dtype=jnp.int32)[None, None, :]
-    ).astype(jnp.float32)
-    gate_values = jnp.sum(route_onehot * router_probs[:, None, :], -1).astype(jnp.bfloat16)
-    shared_gate_b = shared_gate.astype(jnp.bfloat16)
-    shared_prob = jax.nn.sigmoid(
-        jnp.dot(second_in, shared_gate_b, preferred_element_type=jnp.float32)
-    )
-    shared_scale = shared_prob.astype(jnp.bfloat16)
-    slot_index, slot_owner = slot_table(routes)
-    slot_gate = (
-        jnp.zeros((EXPERTS * CAP,), jnp.float32)
-        .at[slot_index]
-        .set(gate_values.reshape(-1).astype(jnp.float32))
-    )
-    owner_grid = slot_owner.reshape(EXPERTS, CAP)
-    gate_grid = slot_gate.reshape(EXPERTS, CAP)
-    padded_in = jnp.concatenate([second_in, jnp.zeros((1, model_width), jnp.bfloat16)], 0)
-
-    def fetch_expert(expert_index):
-        gate_up = lax.dynamic_index_in_dim(expert_gate_up, expert_index, 0, keepdims=False).astype(
-            jnp.bfloat16
-        )
-        down_rows = lax.dynamic_index_in_dim(expert_down, expert_index, 0, keepdims=False).astype(
-            jnp.bfloat16
-        )
-        return (
-            lax.all_gather(gate_up, "dp", axis=2, tiled=True),
-            lax.all_gather(down_rows, "dp", axis=1, tiled=True),
-        )
-
-    def expert_forward(combined, expert_index):
-        gate_up, down_rows = fetch_expert(expert_index)
-        takers = owner_grid[expert_index]
-        taken = padded_in[takers]
-        pre_act = jnp.einsum("cd,jfd->cjf", taken, gate_up, preferred_element_type=jnp.float32)
-        hidden = (jax.nn.silu(pre_act[:, 0]) * pre_act[:, 1]).astype(jnp.bfloat16)
-        result = jnp.einsum("cf,fd->cd", hidden, down_rows, preferred_element_type=jnp.float32)
-        combined = combined.at[takers].add(result * gate_grid[expert_index][:, None])
-        stored = (pre_act,)
-        return (combined, stored)
+    grad_rows = lax.all_gather(cotangent, "tensor", axis=0, tiled=True)
+    gate_rows = jnp.concatenate([router, shared_gate[None, :]], 0).astype(jnp.bfloat16)
+    logits = jnp.einsum("ed,td->et", gate_rows, second_in, preferred_element_type=jnp.float32)
+    router_probs = jax.nn.softmax(logits[:EXPERTS], 0)
+    shared_prob = jax.nn.sigmoid(logits[EXPERTS])
+    shared_scale = shared_prob.astype(jnp.bfloat16).astype(jnp.float32)
+    gate_values = router_probs.astype(jnp.bfloat16)
 
     expert_ids = jnp.arange(EXPERTS, dtype=jnp.int32)
-    combined, stored = lax.scan(
-        expert_forward, jnp.zeros((BLOCK + 1, model_width), jnp.float32), expert_ids
-    )
+    named = jnp.any(routes.T[:, None, :] == expert_ids[None, :, None], 0)
+    row_ids = jnp.arange(BLOCK, dtype=jnp.int32)
+    before = (row_ids[:, None] < row_ids[None, :]).astype(jnp.bfloat16)
+    rank_in = jnp.einsum(
+        "et,ts->es", named.astype(jnp.bfloat16), before, preferred_element_type=jnp.float32
+    ).astype(jnp.int32)
+    share = -(-CAP // (8 * tensor_count)) * 8
+    slots = EXPERTS * share
+    slot_ids = jnp.arange(share, dtype=jnp.int32) + share * lax.axis_index("tensor")
+    owned = named[:, None, :] & (rank_in[:, None, :] == slot_ids[None, :, None])
+    pick = owned.astype(jnp.bfloat16).reshape(slots, BLOCK)
+    slot_gate = jnp.sum(
+        jnp.where(owned, gate_values[:, None, :], 0).astype(jnp.float32), -1
+    ).reshape(slots, 1)
+    members = groups[2]
+    taken_send = jnp.einsum("mt,td->md", pick, second_in, preferred_element_type=jnp.float32)
+    taken = swap_groups(
+        taken_send.astype(jnp.bfloat16).reshape(EXPERTS, share, model_width), members
+    ).reshape(slots, model_width)
+    slot_cot = jnp.einsum("mt,td->md", pick, grad_rows, preferred_element_type=jnp.float32)
+    result_grad = swap_groups(
+        (slot_cot * slot_gate).astype(jnp.bfloat16).reshape(EXPERTS, share, model_width), members
+    ).reshape(slots, model_width)
+    slot_cot = slot_cot.astype(jnp.bfloat16)
+
+    pre_act = jnp.einsum(
+        "cd,jfd->cjf", taken, expert_rows[:2], preferred_element_type=jnp.float32
+    )
+    hidden = (jax.nn.silu(pre_act[:, 0]) * pre_act[:, 1]).astype(jnp.bfloat16)
+    result = jnp.einsum("cf,fd->cd", hidden, expert_rows[2], preferred_element_type=jnp.float32)
+    result_back = swap_groups(
+        result.astype(jnp.bfloat16).reshape(EXPERTS, share, model_width), members
+    ).reshape(slots, model_width)
+    hidden_grad = jnp.einsum(
+        "cd,fd->cf", result_grad, expert_rows[2], preferred_element_type=jnp.float32
+    )
+    pre_grad = silu_back(pre_act, hidden_grad).astype(jnp.bfloat16)
+    rows_grad = jnp.einsum(
+        "cjf,jfd->cd", pre_grad, expert_rows[:2], preferred_element_type=jnp.float32
+    )
+    rows_back = swap_groups(
+        rows_grad.astype(jnp.bfloat16).reshape(EXPERTS, share, model_width), members
+    ).reshape(slots, model_width)
+    gate_up_part = jnp.einsum("cjf,cd->jfd", pre_grad, taken, preferred_element_type=jnp.float32)
+    down_part = jnp.einsum("cf,cd->fd", hidden, result_grad, preferred_element_type=jnp.float32)
+    expert_gate_up_grad, expert_down_grad = return_expert_grads(
+        jnp.concatenate([gate_up_part.astype(jnp.bfloat16), down_part.astype(jnp.bfloat16)[None]], 0),
+        groups,
+    )
+
     shared_pre = jnp.einsum(
         "td,djf->tjf", second_in, shared_up_full, preferred_element_type=jnp.float32
     )
@@ -266,67 +330,23 @@
     shared_result = jnp.einsum(
         "tf,df->td", shared_hidden, shared_down_full, preferred_element_type=jnp.float32
     )
-    mixed_part = combined[:BLOCK] + shared_scale.astype(jnp.float32)[:, None] * shared_result
-    mixed_local = lax.psum_scatter(
-        mixed_part.astype(jnp.bfloat16), "tensor", scatter_dimension=0, tiled=True
-    ).astype(jnp.float32)
+    gated_pick = pick * slot_gate.astype(jnp.bfloat16)
+    combined = jnp.einsum("mt,md->td", gated_pick, result_back, preferred_element_type=jnp.float32)
+    mixed_part = combined + shared_scale[:, None] * shared_result
+    mixed_local = sum_over_tensor(mixed_part.astype(jnp.bfloat16))
     layer_out = (middle + mixed_local).astype(jnp.bfloat16)
-    grad_rows = lax.all_gather(cotangent, "tensor", axis=0, tiled=True)
-    padded_grad = jnp.concatenate([grad_rows, jnp.zeros((1, model_width), jnp.bfloat16)], 0)
-
-    def expert_backward(running, scanned):
-        grad_second, slot_grad = running
-        expert_index = scanned[0]
-        pre_act = scanned[1]
-        gate_up, down_rows = fetch_expert(expert_index)
-        takers = owner_grid[expert_index]
-        taken = padded_in[takers]
-        taken_grad = padded_grad[takers].astype(jnp.float32)
-        hidden = (jax.nn.silu(pre_act[:, 0]) * pre_act[:, 1]).astype(jnp.bfloat16)
-        result = jnp.einsum("cf,fd->cd", hidden, down_rows, preferred_element_type=jnp.float32)
-        slot_grad = slot_grad.at[expert_index].set(jnp.sum(taken_grad * result, -1))
-        result_grad = (gate_grid[expert_index][:, None] * taken_grad).astype(jnp.bfloat16)
-        hidden_grad = jnp.einsum(
-            "cd,fd->cf", result_grad, down_rows, preferred_element_type=jnp.float32
-        )
-        pre_grad = silu_back(pre_act, hidden_grad).astype(jnp.bfloat16)
-        rows_back = jnp.einsum("cjf,jfd->cd", pre_grad, gate_up, preferred_element_type=jnp.float32)
-        grad_second = grad_second.at[takers].add(rows_back)
-        first_part = jnp.einsum("cd,cjf->djf", taken, pre_grad, preferred_element_type=jnp.float32)
-        second_part = jnp.einsum(
-            "cd,cf->df", result_grad, hidden, preferred_element_type=jnp.float32
-        )
-        weight_grad = lax.psum_scatter(
-            jnp.concatenate([first_part, second_part[:, None]], 1).astype(jnp.bfloat16),
-            "dp",
-            scatter_dimension=0,
-            tiled=True,
-        ).astype(jnp.float32)
-        return ((grad_second, slot_grad), weight_grad)
-
-    start_state = (
-        jnp.zeros((BLOCK + 1, model_width), jnp.float32),
-        jnp.zeros((EXPERTS, CAP), jnp.float32),
-    )
-    (grad_second, slot_grad), weight_grads = lax.scan(
-        expert_backward, start_state, (expert_ids,) + stored
-    )
-    expert_gate_up_grad = jnp.transpose(weight_grads[:, :, :2], (0, 2, 3, 1))
-    expert_down_grad = jnp.transpose(weight_grads[:, :, 2], (0, 2, 1))
-    gate_grad = slot_grad.reshape(-1)[slot_index].reshape(BLOCK, TOP)
-    prob_grad = jnp.sum(route_onehot * gate_grad[:, :, None], 1)
-    logit_grad = router_probs * (prob_grad - jnp.sum(router_probs * prob_grad, -1, keepdims=True))
-    router_part = jnp.einsum(
-        "td,te->de", second_in, logit_grad, precision=HIGHEST, preferred_element_type=jnp.float32
-    )
-    grad_second = grad_second[:BLOCK] + jnp.dot(
-        logit_grad, router_b.astype(jnp.float32), precision=HIGHEST
-    )
+
+    slot_grad = jnp.sum(slot_cot.astype(jnp.float32) * result_back.astype(jnp.float32), -1)
+    prob_grad = jnp.sum(jnp.where(owned, slot_grad.reshape(EXPERTS, share, 1), 0.0), 1)
+    logit_grad = router_probs * (prob_grad - jnp.sum(router_probs * prob_grad, 0, keepdims=True))
     grad_rows_f = grad_rows.astype(jnp.float32)
     shared_scale_grad = jnp.sum(grad_rows_f * shared_result, -1)
-    shared_result_grad = (shared_scale.astype(jnp.float32)[:, None] * grad_rows_f).astype(
-        jnp.bfloat16
-    )
+    shared_logit_grad = shared_scale_grad * shared_prob * (1.0 - shared_prob)
+    logit_grads = jnp.concatenate([logit_grad, shared_logit_grad[None, :]], 0).astype(jnp.bfloat16)
+    gate_rows_part = jnp.einsum(
+        "et,td->ed", logit_grads, second_in, preferred_element_type=jnp.float32
+    )
+    shared_result_grad = (shared_scale[:, None] * grad_rows_f).astype(jnp.bfloat16)
     shared_hidden_grad = jnp.einsum(
         "td,df->tf", shared_result_grad, shared_down_full, preferred_element_type=jnp.float32
     )
@@ -337,31 +357,16 @@
     shared_up_part = jnp.einsum(
         "td,tjf->djf", second_in, shared_pre_grad, preferred_element_type=jnp.float32
     )
+    grad_second = jnp.einsum(
+        "tjf,djf->td", shared_pre_grad, shared_up_full, preferred_element_type=jnp.float32
+    )
     grad_second = grad_second + jnp.einsum(
-        "tjf,djf->td", shared_pre_grad, shared_up_full, preferred_element_type=jnp.float32
-    )
-    shared_logit_grad = shared_scale_grad * shared_prob * (1.0 - shared_prob)
-    shared_gate_part = jnp.einsum(
-        "td,t->d",
-        second_in,
-        shared_logit_grad,
-        precision=HIGHEST,
-        preferred_element_type=jnp.float32,
-    )
-    grad_second = (
-        grad_second + shared_logit_grad[:, None] * shared_gate_b.astype(jnp.float32)[None, :]
-    )
-    router_spread = jnp.transpose(spread_rows(router_part, dp_count, tensor_count))
-    second_grad, router_share, shared_gate_share = (
-        lax.psum_scatter(grad_second, "tensor", scatter_dimension=0, tiled=True),
-        lax.psum_scatter(router_spread, "tensor", scatter_dimension=1, tiled=True),
-        lax.psum_scatter(
-            spread_rows(shared_gate_part, dp_count, tensor_count),
-            "tensor",
-            scatter_dimension=0,
-            tiled=True,
-        ),
-    )
+        "et,ed->td", logit_grads, gate_rows, preferred_element_type=jnp.float32
+    )
+    grad_second = grad_second + jnp.einsum(
+        "mt,md->td", pick, rows_back, preferred_element_type=jnp.float32
+    )
+    second_grad = sum_over_tensor(grad_second.astype(jnp.bfloat16))
     gain_ffn_part = jnp.sum(second_grad * normed_second, 0)
     middle_grad = cotangent.astype(jnp.float32) + norm_back(
         second_grad, normed_second, factor_second, gain_ffn
@@ -441,22 +446,15 @@
         "tjh,djh->td", qkv_grad, qkv_full, preferred_element_type=jnp.float32
     )
     gain_attn_part = jnp.sum(first_grad_part * normed_first, 0)
-    first_grad, gain_attn_share, gain_ffn_share = (
-        lax.psum_scatter(
-            first_grad_part.astype(jnp.bfloat16), "tensor", scatter_dimension=0, tiled=True
-        ).astype(jnp.float32),
-        lax.psum_scatter(
-            spread_rows(gain_attn_part, dp_count, tensor_count).astype(jnp.bfloat16),
-            "tensor",
-            scatter_dimension=0,
-            tiled=True,
-        ).astype(jnp.float32),
-        lax.psum_scatter(
-            spread_rows(gain_ffn_part, dp_count, tensor_count).astype(jnp.bfloat16),
-            "tensor",
-            scatter_dimension=0,
-            tiled=True,
-        ).astype(jnp.float32),
+    first_grad = sum_over_tensor(first_grad_part.astype(jnp.bfloat16))
+    gate_share = lax.psum_scatter(
+        jnp.concatenate([gate_rows_part, gain_ffn_part[None, :]], 0),
+        ("dp", "tensor"),
+        scatter_dimension=1,
+        tiled=True,
+    )
+    gain_attn_share = lax.psum_scatter(
+        gain_attn_part, ("dp", "tensor"), scatter_dimension=0, tiled=True
     )
     normed_local = lax.dynamic_slice_in_dim(normed_first, row_start, tok_rows, 0)
     factor_local = lax.dynamic_slice_in_dim(factor_first, row_start, tok_rows, 0)
@@ -477,29 +475,17 @@
         lax.psum_scatter(
             shared_down_part.astype(jnp.bfloat16), "dp", scatter_dimension=0, tiled=True
         ).astype(jnp.float32),
-        lax.psum_scatter(
-            gain_attn_share.astype(jnp.bfloat16), "dp", scatter_dimension=0, tiled=True
-        ).astype(jnp.float32),
-        lax.psum_scatter(
-            gain_ffn_share.astype(jnp.bfloat16), "dp", scatter_dimension=0, tiled=True
-        ).astype(jnp.float32),
-        lax.psum_scatter(
-            router_share.astype(jnp.bfloat16), "dp", scatter_dimension=1, tiled=True
-        ).astype(jnp.float32),
-        lax.psum_scatter(
-            shared_gate_share.astype(jnp.bfloat16), "dp", scatter_dimension=0, tiled=True
-        ).astype(jnp.float32),
     )
     return (
         layer_out,
         input_grad,
-        summed[5],
+        gain_attn_share,
         summed[0],
         summed[2],
         summed[1],
-        summed[6],
-        summed[7],
-        summed[8],
+        gate_share[EXPERTS + 1],
+        gate_share[:EXPERTS],
+        gate_share[EXPERTS],
         expert_gate_up_grad,
         expert_down_grad,
         summed[3],

time: 5120 us -> 2460 us (0.48)
  waiting for transfers between devices: 2520 us -> 854 us
  local copies, waits for them, and re-layouts: 868 us -> 319 us
  other arithmetic: 808 us -> 306 us
  starting transfers between devices: 4.59 us -> 169 us
  matrix products: 752 us -> 626 us
  blocking collectives: 48.7 us -> 144 us
  loops' own time: 79.6 us -> 12.7 us
    all_gather x64 -> x0, waiting for transfers between devices: 1250 us -> none  [the longest x32 819 us: fetch_expert(): lax.all_gather(gate_up, 'dp', axis=2, tiled=True)]
    reduce_scatter x21 -> x0, waiting for transfers between devices: 917 us -> none  [the longest x16 526 us: expert_backward(): lax.psum_scatter(jnp.concatenate([first_part, second_part[:, None]], 1).a...]
    all_to_all x0 -> x9, waiting for transfers between devices: none -> 680 us  [the longest x6 600 us: swap_groups(): lax.all_to_all(value, ('dp', 'tensor'), split_axis=0, concat_axis=0, tile...]
    scatter-add x32 -> x0, other arithmetic: 483 us -> none  [the longest x16 244 us: expert_backward(): grad_second = grad_second.at[takers].add(rows_back)]
    gather x49 -> x0, local copies, waits for them, and re-layouts: 419 us -> none  [the longest x16 128 us: expert_backward(): taken = padded_in[takers]]
    all_to_all x0 -> x9, starting transfers between devices: none -> 168 us  [the longest x6 143 us: swap_groups(): lax.all_to_all(value, ('dp', 'tensor'), split_axis=0, concat_axis=0, tile...]
    dot_general x117 -> x14, matrix products: 336 us -> 217 us  [the longest x1 27.9 us: local(): jnp.einsum('cjf,cd->jfd', pre_grad, taken, preferred_element_type=jnp.flo...]
    convert_element_type x73 -> x0, local copies, waits for them, and re-layouts: 108 us -> none  [the longest x32 55.9 us: fetch_expert(): lax.dynamic_index_in_dim(expert_gate_up, expert_index, 0, keepdims=False)]
  transfers between devices with their start and end apart: 103 -> 29, of which waited for: 93 -> 12; matrix products, arithmetic and copies ran while one was open for 36% -> 47% of each run, Pallas kernels for 0% -> 0%
where the time goes in v1:
time: 2460 us; the launch traced here: 2450 us
  waiting for transfers between devices  854 us (35%)
  matrix products  626 us (25%)
  local copies, waits for them, and re-layouts  319 us (13%)
  other arithmetic  306 us (12%)
  starting transfers between devices  169 us (7%)
  blocking collectives  144 us (6%)
    all_to_all x6, waiting for transfers between devices, swap_groups(): lax.all_to_all(value, ('dp', 'tensor'), split_axis=0, concat_axis=0, tile...  600 us
    all_to_all x6, starting transfers between devices, swap_groups(): lax.all_to_all(value, ('dp', 'tensor'), split_axis=0, concat_axis=0, tile...  143 us
    all_to_all x1, blocking collectives, sum_over_tensor(): lax.all_to_all(value, 'tensor', split_axis=0, concat_axis=0, tiled=True)  81.1 us
    all_to_all x3, waiting for transfers between devices, sum_over_tensor(): lax.all_to_all(value, 'tensor', split_axis=0, concat_axis=0, tiled=True)  80.2 us
    all_gather x1, waiting for transfers between devices, local(): lax.all_gather(w_qkv.astype(jnp.bfloat16), 'dp', axis=0, tiled=True)  63.2 us
    dot_general x6, matrix products, block_scores(): jnp.einsum('qhd,khd->hqk', query_rows, key_all, preferred_element_type=jn...  58 us
    all_gather x1, waiting for transfers between devices, local(): block_in = lax.all_gather(inputs, 'tensor', axis=0, tiled=True)  51.5 us
  transfers between devices with their start and end apart: 29, of which 12 were waited for; matrix products, arithmetic and copies ran while one was open for 47% of the time, Pallas kernels for 0%

profile of v1, /device:TPU:0, one launch (start us, length us, event | category | flops | bytes accessed | tf_op | source)
XLA Modules:
  0.0 2446.9 jit_solution(10386579008236729549)
XLA Ops:
  31.1 51.5 %all-gather.9.cloned.1.call-done = bf16[1536,2048]{1,0:T(8,128)(2,1)} async-done(((bf16[384,2048]{1,0:T(8,128)(2,1)}), bf16[1536,2048]{1,0:T(8,128)(2,1)}) %all-gather.9.cloned.1.call-update) | async-done | bytes 6291472 | tf_op jit(solution)/shard_map/all_gather | solution.py:200
  86.7 63.2 %all-gather.11.cloned.1.call-done = bf16[2048,3,512]{0,2,1:T(8,128)(2,1)} async-done(((bf16[256,3,512]{0,2,1:T(8,128)(2,1)}), bf16[2048,3,512]{0,2,1:T(8,128)(2,1)}) %all-gather.11.cloned.1.call-update) | async-done | bytes 6291472 | tf_op jit(solution)/shard_map/all_gather | solution.py:190
  212.7 106.3 %while.31 = (s32[]{:T(128)}, bf16[3,512,4,128]{1,3,2,0:T(8,128)(2,1)}, f32[3,4,512]{2,1,0:T(4,128)}, s32[3]{0:T(128)S(1)}, bf16[1536,4,128]{0,2,1:T(8,128)(2,1)}...) while((s32[]{:T(128)}, ...), condition=%wide.region_4.5_spmd, body=%wide.region_1.4_spmd.sunk | while | flops 2762209792 | bytes 163660512 | solution.py:256
  361.2 52.9 %all-to-all-done = bf16[4,384,2048]{2,1,0:T(8,128)(2,1)} async-done(((bf16[4,384,2048]{2,1,0:T(8,128)(2,1)}), bf16[4,384,2048]{2,1,0:T(8,128)(2,1)}, u32[]{:S(2)}, u32[]{:S(2)}) %all-to-all-start) | async-done | bytes 6291488 | tf_op jit(solution)/shard_map/all_to_all | solution.py:90
  430.9 151.8 %all-to-all-done.2 = bf16[16,1056,256]{2,1,0:T(8,128)(2,1)} async-done(((bf16[16,1056,256]{2,1,0:T(8,128)(2,1)}), bf16[16,1056,256]{2,1,0:T(8,128)(2,1)}, u32[]{:S(2)}, u32[]{:S(2)}) %all-to-all-start.2) | async-done | bytes 8650784 | tf_op jit(solution)/shard_map/all_to_all | solution.py:83
  609.5 25.7 %all-to-all-start.1 = ((bf16[16,104,2048]{2,1,0:T(8,128)(2,1)}), bf16[16,104,2048]{2,1,0:T(8,128)(2,1)}, u32[]{:S(2)}, u32[]{:S(2)}) async-start(bf16[16,104,2048]{2,1,0:T(8,128)(2,1)} %bitcast.285), calls=%async_computation.1 | async-start | bytes 13631488 | tf_op jit(solution)/shard_map/all_to_all | solution.py:83
  723.9 43.3 %all-to-all-done.1 = bf16[16,104,2048]{2,1,0:T(8,128)(2,1)} async-done(((bf16[16,104,2048]{2,1,0:T(8,128)(2,1)}), bf16[16,104,2048]{2,1,0:T(8,128)(2,1)}, u32[]{:S(2)}, u32[]{:S(2)}) %all-to-all-start.1) | async-done | bytes 6815776 | tf_op jit(solution)/shard_map/all_to_all | solution.py:83
  767.1 26.2 %fusion.145 = f32[1664,2,1408]{2,0,1:T(8,128)S(1)} fusion(bf16[1664,2048,1]{1,0,2:T(8,128)(2,1)} %bitcast.15, bf16[2,1408,2048]{2,1,0:T(8,128)(2,1)} %slice.170), kind=kOutput, calls=%fused_computation.282 | convolution fusion | flops 19193135104 | bytes 37093376 | tf_op jit(solution)/shard_map/cd,jfd->cjf/dot_general | solution.py:301
  814.1 30.1 %all-to-all-start.3 = ((bf16[16,104,2048]{2,1,0:T(8,128)(2,1)}), bf16[16,104,2048]{2,1,0:T(8,128)(2,1)}, u32[]{:S(2)}, u32[]{:S(2)}) async-start(bf16[16,104,2048]{2,1,0:T(8,128)(2,1)} %bitcast.286), calls=%async_computation.3 | async-start | bytes 13631488 | tf_op jit(solution)/shard_map/all_to_all | solution.py:83
  852.3 208.5 %all-to-all-done.3 = bf16[16,104,2048]{2,1,0:T(8,128)(2,1)} async-done(((bf16[16,104,2048]{2,1,0:T(8,128)(2,1)}), bf16[16,104,2048]{2,1,0:T(8,128)(2,1)}, u32[]{:S(2)}, u32[]{:S(2)}) %all-to-all-start.3) | async-done | bytes 6815776 | tf_op jit(solution)/shard_map/all_to_all | solution.py:83
  1090.7 30.8 %all-to-all-start.5 = ((bf16[16,104,2048]{2,1,0:T(8,128)(2,1)}), bf16[16,104,2048]{2,1,0:T(8,128)(2,1)}, u32[]{:S(2)}, u32[]{:S(2)}) async-start(bf16[16,104,2048]{2,1,0:T(8,128)(2,1)} %bitcast.275), calls=%async_computation.5 | async-start | bytes 13631488 | tf_op jit(solution)/shard_map/all_to_all | solution.py:83
  1122.5 26.2 %fusion.75 = f32[1536,2,1408]{2,0,1:T(8,128)} fusion(bf16[2048,2,1408]{2,0,1:T(8,128)(2,1)} %all-gather.17.cloned.1.call-done, bf16[1536,2048]{1,0:T(8,128)(2,1)} %all-gather.15.cloned.1.call-done), kind=kOutput, calls=%fused_computation.147 | convolution fusion | flops 17716740096 | bytes 35127296 | tf_op jit(solution)/shard_map/td,djf->tjf/dot_general | solution.py:326
  1148.7 142.7 %all-to-all-done.5 = bf16[16,104,2048]{2,1,0:T(8,128)(2,1)} async-done(((bf16[16,104,2048]{2,1,0:T(8,128)(2,1)}), bf16[16,104,2048]{2,1,0:T(8,128)(2,1)}, u32[]{:S(2)}, u32[]{:S(2)}) %all-to-all-start.5) | async-done | bytes 6815776 | tf_op jit(solution)/shard_map/all_to_all | solution.py:83
  1314.6 26.2 %bitcast_convert_fusion = bf16[1664,2048]{1,0:T(8,128)(2,1)} fusion(bf16[2,1408,2048]{2,1,0:T(8,128)(2,1)} %slice.170, bf16[1664,1,1408]{2,0,1:T(8,128)(2,1)} %get-tuple-element.570, bf16[1664,1,1408]{2,0,1:T(8,128)(2,1)} %get-tuple-element.569), kind=kOutput, calls=%fused_computation.82 | convolution fusion | flops 19201228800 | bytes 27721728 | tf_op jit(solution)/shard_map/cjf,jfd->cd/dot_general | solution.py:313
  1340.9 29.9 %all-to-all-start.6 = ((bf16[16,104,2048]{2,1,0:T(8,128)(2,1)}), bf16[16,104,2048]{2,1,0:T(8,128)(2,1)}, u32[]{:S(2)}, u32[]{:S(2)}) async-start(bf16[16,104,2048]{2,1,0:T(8,128)(2,1)} %bitcast.284), calls=%async_computation.6 | async-start | bytes 13631488 | tf_op jit(solution)/shard_map/all_to_all | solution.py:83
  1417.7 25.3 %fusion.77 = f32[1536,2048,1]{1,0,2:T(8,128)} fusion(bf16[2048,2,1408]{2,0,1:T(8,128)(2,1)} %all-gather.17.cloned.1.call-done, bf16[1536,1,1408]{2,0,1:T(8,128)(2,1)} %get-tuple-element.572, bf16[1536,1,1408]{2,0,1:T(8,128)(2,1)} %get-tuple-element.571), kind=kOutput, calls=%fused_computation.150 | convolution fusion | flops 17721065472 | bytes 32768000 | tf_op jit(solution)/shard_map/tjf,djf->td/dot_general | solution.py:360
  1443.1 53.4 %all-to-all-done.6 = bf16[16,104,2048]{2,1,0:T(8,128)(2,1)} async-done(((bf16[16,104,2048]{2,1,0:T(8,128)(2,1)}), bf16[16,104,2048]{2,1,0:T(8,128)(2,1)}, u32[]{:S(2)}, u32[]{:S(2)}) %all-to-all-start.6) | async-done | bytes 6815776 | tf_op jit(solution)/shard_map/all_to_all | solution.py:83
  1523.4 81.1 %all_to_all.66 = bf16[4,384,2048]{2,1,0:T(8,128)(2,1)S(1)} all-to-all(bf16[4,384,2048]{2,1,0:T(8,128)(2,1)S(1)} %bitcast.278), channel_id=1, replica_groups=mesh['dp'=8,'tensor'=4] {'tensor'}, dimensions={0} | all-to-all | bytes 12582912 | tf_op jit(solution)/shard_map/all_to_all | solution.py:90
  1626.4 27.9 %convolution_convert_fusion.1 = bf16[2,1408,2048]{2,1,0:T(8,128)(2,1)} fusion(bf16[1664,2048,1]{1,0,2:T(8,128)(2,1)} %bitcast.15, bf16[1664,1,1408]{2,0,1:T(8,128)(2,1)} %get-tuple-element.570, bf16[1664,1,1408]{2,0,1:T(8,128)(2,1)} %get-tuple-element.569), kind=kOutput, calls=%fused_computation.101 | convolution fusion | flops 19203588096 | bytes 27721728 | tf_op jit(solution)/shard_map/cjf,cd->jfd/dot_general | solution.py:319
  1748.3 25.0 %convolution_convert_fusion = bf16[2048,2,1408]{2,0,1:T(8,128)(2,1)} fusion(bf16[1536,2048]{1,0:T(8,128)(2,1)} %all-gather.15.cloned.1.call-done, bf16[1536,1,1408]{2,0,1:T(8,128)(2,1)} %get-tuple-element.572, bf16[1536,1,1408]{2,0,1:T(8,128)(2,1)} %get-tuple-element.571), kind=kOutput, calls=%fused_computation.100 | convolution fusion | flops 17739808768 | bytes 26476544 | tf_op jit(solution)/shard_map/td,tjf->djf/dot_general | solution.py:357
  1791.8 27.3 %all-to-all-done.4 = bf16[4,384,2048]{2,1,0:T(8,128)(2,1)} async-done(((bf16[4,384,2048]{2,1,0:T(8,128)(2,1)}), bf16[4,384,2048]{2,1,0:T(8,128)(2,1)}, u32[]{:S(2)}, u32[]{:S(2)}) %all-to-all-start.4) | async-done | bytes 6291488 | tf_op jit(solution)/shard_map/all_to_all | solution.py:90
  1844.6 303.3 %while.32 = (s32[]{:T(128)}, f32[2048,4,128]{0,2,1:T(8,128)}, f32[2048,4,128]{0,2,1:T(8,128)}, f32[3,512,4,128]{3,1,0,2:T(8,128)}, f32[3,512,4,128]{1,3,2,0:T(8,...) while((s32[]{:T(128)}, f32[2048,4,128]{0,2,1:T(8,128)}, ...), condition=%wide.region_20.21_spmd.clone, body=%wide.region_18.20_spmd.clone.sunk | while | flops 6815480320 | bytes 323036096 | solution.py:411
  2337.6 47.0 %all-reduce = f32[2048]{0:T(1024)S(1)} all-reduce(f32[2048]{0:T(1024)S(1)} %get-tuple-element.583), channel_id=2, replica_groups=mesh['dp'=8,'tensor'=4] {'dp','tensor'}, use_global_device_ids=true, to_apply=%region_24.25.clone | all-reduce | flops 2048 | bytes 16384
  2401.8 35.7 %reduce-scatter.11.cloned.1.call-done = bf16[256,3,512]{2,0,1:T(8,128)(2,1)} async-done(((bf16[2048,3,512]{2,0,1:T(8,128)(2,1)}), bf16[256,3,512]{2,0,1:T(8,128)(2,1)}) %reduce-scatter.11.cloned.1.call-update) | async-done | bytes 786448 | tf_op jit(solution)/shard_map/reduce_scatter | solution.py:463
  (542 shorter events, 1186.8 us)
Async XLA Ops:
  7.2 75.4 %all-gather.9.cloned.1.call-start = ((), (), s32[]{:S(2)}) async-start(), calls=%async_computation.16 | async-start | bytes 7864320 | tf_op jit(solution)/shard_map/all_gather | solution.py:200
  7.9 142.0 %all-gather.11.cloned.1.call-start = ((), (), s32[]{:S(2)}) async-start(), calls=%async_computation.17 | async-start | bytes 7077888 | tf_op jit(solution)/shard_map/all_gather | solution.py:190
  10.6 311.2 %all-gather.13.cloned.1.call-start = ((), (), s32[]{:S(2)}) async-start(), calls=%async_computation.18 | async-start | bytes 2359296 | tf_op jit(solution)/shard_map/all_gather | solution.py:191
  329.3 84.8 %all-to-all-start = ((bf16[4,384,2048]{2,1,0:T(8,128)(2,1)}), bf16[4,384,2048]{2,1,0:T(8,128)(2,1)}, u32[]{:S(2)}, u32[]{:S(2)}) async-start(bf16[4,384,2048]{2,1,0:T(8,128)(2,1)} %bitcast.289), calls=%async_computation | async-start | bytes 12582912 | tf_op jit(solution)/shard_map/all_to_all | solution.py:90
  414.2 168.5 %all-to-all-start.2 = ((bf16[16,1056,256]{2,1,0:T(8,128)(2,1)}), bf16[16,1056,256]{2,1,0:T(8,128)(2,1)}, u32[]{:S(2)}, u32[]{:S(2)}) async-start(bf16[16,1056,256]{2,1,0:T(8,128)(2,1)} %bitcast.273), calls=%async_computation.2 | async-start | bytes 17301504 | tf_op jit(solution)/shard_map/all_to_all | solution.py:83
  418.9 176.0 %all-gather.15.cloned.1.call-start = ((), (), s32[]{:S(2)}) async-start(), calls=%async_computation.19 | async-start | bytes 7864320 | tf_op jit(solution)/shard_map/all_gather | solution.py:266
  582.7 53.1 %collective-permute-start.2 = (bf16[16,1056,256]{2,1,0:T(8,128)(2,1)}, bf16[16,1056,256]{2,1,0:T(8,128)(2,1)}, u32[]{:S(2)}, u32[]{:S(2)}) collective-permute-start(bf16[16,1056,256]{2,1,0:T(8,128)(2,1)} %all-to-all-done.2), channel_id=1, source_target_pairs={{0,4},{4,0},{8,12},{12,8},{16,20},{20,16},{24,28},{28,24},{1,5},{5... | collective-permute-start | bytes 25952264 | tf_op jit(solution)/shard_map/ppermute | solution.py:106
  609.5 157.6 %all-to-all-start.1 = ((bf16[16,104,2048]{2,1,0:T(8,128)(2,1)}), bf16[16,104,2048]{2,1,0:T(8,128)(2,1)}, u32[]{:S(2)}, u32[]{:S(2)}) async-start(bf16[16,104,2048]{2,1,0:T(8,128)(2,1)} %bitcast.285), calls=%async_computation.1 | async-start | bytes 13631488 | tf_op jit(solution)/shard_map/all_to_all | solution.py:83
  635.2 217.0 %all-gather.21.cloned.1.call-start = ((), (), s32[]{:S(2)}) async-start(), calls=%async_computation.22 | async-start | bytes 7864320 | tf_op jit(solution)/shard_map/all_gather | solution.py:267
  814.1 246.6 %all-to-all-start.3 = ((bf16[16,104,2048]{2,1,0:T(8,128)(2,1)}), bf16[16,104,2048]{2,1,0:T(8,128)(2,1)}, u32[]{:S(2)}, u32[]{:S(2)}) async-start(bf16[16,104,2048]{2,1,0:T(8,128)(2,1)} %bitcast.286), calls=%async_computation.3 | async-start | bytes 13631488 | tf_op jit(solution)/shard_map/all_to_all | solution.py:83
  844.3 278.3 %all-gather.17.cloned.1.call-start = ((), (), s32[]{:S(2)}) async-start(), calls=%async_computation.20 | async-start | bytes 12976128 | tf_op jit(solution)/shard_map/all_gather | solution.py:193
  1090.7 200.7 %all-to-all-start.5 = ((bf16[16,104,2048]{2,1,0:T(8,128)(2,1)}), bf16[16,104,2048]{2,1,0:T(8,128)(2,1)}, u32[]{:S(2)}, u32[]{:S(2)}) async-start(bf16[16,104,2048]{2,1,0:T(8,128)(2,1)} %bitcast.275), calls=%async_computation.5 | async-start | bytes 13631488 | tf_op jit(solution)/shard_map/all_to_all | solution.py:83
  1121.5 258.5 %all-gather.19.cloned.1.call-start = ((), (), s32[]{:S(2)}) async-start(), calls=%async_computation.21 | async-start | bytes 6488064 | tf_op jit(solution)/shard_map/all_gather | solution.py:194
  1340.9 155.6 %all-to-all-start.6 = ((bf16[16,104,2048]{2,1,0:T(8,128)(2,1)}), bf16[16,104,2048]{2,1,0:T(8,128)(2,1)}, u32[]{:S(2)}, u32[]{:S(2)}) async-start(bf16[16,104,2048]{2,1,0:T(8,128)(2,1)} %bitcast.284), calls=%async_computation.6 | async-start | bytes 13631488 | tf_op jit(solution)/shard_map/all_to_all | solution.py:83
  1370.8 412.4 %all-gather.23.cloned.1.call-start = ((), (), s32[]{:S(2)}) async-start(), calls=%async_computation.23 | async-start | bytes 7864320 | tf_op jit(solution)/shard_map/all_gather | solution.py:374
  1611.1 666.7 %reduce-scatter.17.cloned.1.call-start = ((), (), s32[]{:S(2)}) async-start(), calls=%async_computation.27 | async-start | bytes 6488064 | tf_op jit(solution)/shard_map/reduce_scatter | solution.py:475
  1743.0 76.1 %all-to-all-start.4 = ((bf16[4,384,2048]{2,1,0:T(8,128)(2,1)}), bf16[4,384,2048]{2,1,0:T(8,128)(2,1)}, u32[]{:S(2)}, u32[]{:S(2)}) async-start(bf16[4,384,2048]{2,1,0:T(8,128)(2,1)} %bitcast.288), calls=%async_computation.4 | async-start | bytes 12582912 | tf_op jit(solution)/shard_map/all_to_all | solution.py:90
  1748.3 531.9 %reduce-scatter.15.cloned.1.call-start = ((), (), s32[]{:S(2)}) async-start(), calls=%async_computation.26 | async-start | bytes 12976128 | tf_op jit(solution)/shard_map/reduce_scatter | solution.py:472
  1819.1 453.0 %all-to-all-start.9 = ((bf16[16,1056,256]{2,1,0:T(8,128)(2,1)}), bf16[16,1056,256]{2,1,0:T(8,128)(2,1)}, u32[]{:S(2)}, u32[]{:S(2)}) async-start(bf16[16,1056,256]{2,1,0:T(8,128)(2,1)} %fusion.50), calls=%async_computation.11 | async-start | bytes 17301504 | tf_op jit(solution)/shard_map/all_to_all | solution.py:83
  1840.4 460.4 %reduce-scatter.21.cloned.1.call-start = ((), (), s32[]{:S(2)}) async-start(), calls=%async_computation.29 | async-start | bytes 1081344
  2162.0 223.3 %reduce-scatter.19.cloned.1.call-start = ((), (), s32[]{:S(2)}) async-start(), calls=%async_computation.28 | async-start | bytes 36864
  2231.0 155.7 %reduce-scatter.13.cloned.1.call-start = ((), (), s32[]{:S(2)}) async-start(), calls=%async_computation.25 | async-start | bytes 2359296 | tf_op jit(solution)/shard_map/reduce_scatter | solution.py:466
  2239.2 198.3 %reduce-scatter.11.cloned.1.call-start = ((), (), s32[]{:S(2)}) async-start(), calls=%async_computation.24 | async-start | bytes 7077888 | tf_op jit(solution)/shard_map/reduce_scatter | solution.py:463
  2272.1 116.4 %all-to-all-start.8 = ((bf16[4,384,2048]{2,1,0:T(8,128)(2,1)}), bf16[4,384,2048]{2,1,0:T(8,128)(2,1)}, u32[]{:S(2)}, u32[]{:S(2)}) async-start(bf16[4,384,2048]{2,1,0:T(8,128)(2,1)} %bitcast.287), calls=%async_computation.8 | async-start | bytes 12582912 | tf_op jit(solution)/shard_map/all_to_all | solution.py:90
  (116 other events, 2796.6 us)
Sparse Core Ops, SparseCore 0:
  9.8 72.7 all-gather.8
  84.8 65.1 all-gather.10
  195.5 27.3 all-gather.12
  427.3 167.5 all-gather.14
  637.6 144.9 all-gather.20
  846.9 214.6 all-gather.16
  1124.5 144.0 all-gather.18
  1611.2 84.9 all-gather.22
  1698.5 64.7 reduce-scatter.16
  1773.5 244.4 reduce-scatter.14
  2162.1 138.6 reduce-scatter.20
  2303.5 26.5 reduce-scatter.18
  2332.4 34.3 reduce-scatter.12
  2369.0 68.4 reduce-scatter.10
